TPU v7x, 128 devices: a whole 4x4x4 slice. The times are simulated.
128 devices in a mesh: row: 8 (over x, core), col: 16 (over y, z).
Axes of the slice: x: 4, y: 4, z: 4, core: 2. Of those that a mesh axis runs over, the one named last changes fastest.
Arguments:
- coupling: bfloat16 [128, 4096, 1024], P(('row', 'col')), may hold values from -0.09375 to 0.09375
- modes: bfloat16 [128, 200, 4096], P(('row', 'col')), may hold values from -6 to 6
- flexibility: float32 [128, 200], P(('row', 'col')), may hold values from 0.002 to 0.02
- widths: int32 [128], P(('row', 'col')), may hold values from 512 to 1024
- segments: int32 [128, 8], replicated, may hold values from 0 to 95, as said below
Outputs:
- interface: float32 [12288, 12288], P('row', 'col')
Inputs may be any that keep to these rules, and one draw needn't show every extreme that they name: `segments`: the 8 segment numbers of a substructure are distinct, and modulo 16 they are 8 cyclically consecutive residues. `widths`: columns at and beyond a substructure's width are padding.
All inputs are finite; a program needn't handle non-finite values.
Results may differ from a plain program's by a relative error of at most 0.0003.
Values sent between devices are 32-bit elements; how exact they have to be, the bound alone decides.
A program may use at most 192 MiB of HBM per device.

v0:
```python
import functools

import jax
import jax.numpy as jnp
from jax import lax
from jax.experimental import pallas as pl
from jax.experimental.pallas import tpu as pltpu
from jax.sharding import PartitionSpec as P

TILE = 128
PARTS = (16,) * 8
AHEAD = 2
CLASSES = 8
PLANE = 32
RING = 4
ROW_TILES = 12
COL_TILES = 6
DEPTH = 1024
STEPS = 4
SPAN = 64
CAPS = (17, 18, 19, 20, 21, 23, PLANE)
F32 = jnp.float32
BF16 = jnp.bfloat16
MESH = pl.DeviceIdType.MESH
HIGH = lax.Precision.HIGHEST


def over_rows(left, right):
    return lax.dot_general(left, right, (((0,), (0,)), ((), ())), preferred_element_type=F32)


def block_kernel(segments, width, coupling, modes, weights, out, diag, all_wide, *scratch):
    wide, raw, mode_rows, tiles, acc, proj, m_sem, p_sem, w_sem, r_sem, t_sem = scratch
    row, col = lax.axis_index("row"), lax.axis_index("col")
    y, z = col // 4, col % 4
    mine = row * 4 + z

    def plane_peer(step):
        there = lax.rem(mine + step, PLANE)
        return (there // 4, y * 4 + lax.rem(there, 4))

    def ring_peer(step):
        return (row, lax.rem(y + step, RING) * 4 + z)

    def load(k):
        rows = pl.ds(k * DEPTH, DEPTH)
        return pltpu.make_async_copy(coupling.at[0, rows], raw.at[k], m_sem.at[k])

    mode_copy = pltpu.make_async_copy(modes.at[0], mode_rows, p_sem)
    load(0).start()
    mode_copy.start()
    for k in range(1, STEPS):
        load(k).start()
    barrier = pltpu.get_barrier_semaphore()

    def greet(step, carry):
        pl.semaphore_signal(barrier, inc=1, device_id=plane_peer(step), device_id_type=MESH)
        return carry

    lax.fori_loop(1, PLANE, greet, 0)
    for step in range(1, RING):
        pl.semaphore_signal(barrier, inc=1, device_id=ring_peer(step), device_id_type=MESH)
    wide[...] = jnp.zeros((1, TILE), F32) + width[0].astype(F32)
    acc[...] = jnp.zeros_like(acc)
    proj[...] = jnp.zeros_like(proj)
    here = pltpu.make_async_copy(wide, all_wide.at[y, mine], w_sem.at[2])

    def pass_on(step):
        return pltpu.make_async_remote_copy(
            src_ref=all_wide.at[y],
            dst_ref=all_wide.at[y],
            send_sem=r_sem.at[0, step - 1],
            recv_sem=r_sem.at[1, step - 1],
            device_id=ring_peer(step),
            device_id_type=MESH,
        )

    mode_copy.wait()

    def multiply(k, carry):
        load(k).wait()

        @pl.when(k == 1)
        def _():
            pl.semaphore_wait(barrier, PLANE - 1 + RING - 1)

            def tell(step, carry):
                pltpu.make_async_remote_copy(
                    src_ref=wide,
                    dst_ref=all_wide.at[y, mine],
                    send_sem=w_sem.at[0],
                    recv_sem=w_sem.at[1],
                    device_id=plane_peer(step),
                    device_id_type=MESH,
                ).start()
                return carry

            lax.fori_loop(1, PLANE, tell, 0)
            here.start()

        @pl.when(k == STEPS - 1)
        def _():
            others = all_wide.at[y, pl.ds(0, PLANE - 1)]
            pltpu.make_async_copy(others, others, w_sem.at[1]).wait()
            pltpu.make_async_copy(others, others, w_sem.at[0]).wait()
            here.wait()
            for step in range(1, RING):
                pass_on(step).start()

        cols = pl.ds(pl.multiple_of(k * DEPTH, DEPTH), DEPTH)
        proj[...] += jnp.dot(mode_rows[:, cols], raw[k], preferred_element_type=F32)
        for m in range(0, CLASSES, 2):
            part = over_rows(raw[k, :, m * TILE : (m + 2) * TILE], raw[k, :, m * TILE :])
            for i in range(2):
                for n in range(m, CLASSES):
                    inside = part[i * TILE : (i + 1) * TILE, (n - m) * TILE : (n - m + 1) * TILE]
                    acc[m + i, n] += inside
        return carry

    lax.fori_loop(0, STEPS, multiply, 0)
    p = proj[...]
    count = p.shape[0]
    square = lax.broadcasted_iota(jnp.int32, (count, count), 0) == lax.broadcasted_iota(
        jnp.int32, (count, count), 1
    )
    w = p * jnp.sum(jnp.where(square, weights[...], 0.0), axis=1, keepdims=True)
    p_hi, w_hi = p.astype(BF16), w.astype(BF16)
    p_lo = (p - p_hi.astype(F32)).astype(BF16)
    w_lo = (w - w_hi.astype(F32)).astype(BF16)
    left = jnp.concatenate([w_hi, w_hi, w_lo], 0)
    right = jnp.concatenate([p_hi, p_lo, p_hi], 0)
    for m in range(0, CLASSES, 2):
        part = over_rows(left[:, m * TILE : (m + 2) * TILE], right[:, m * TILE :])
        for i in range(2):
            for n in range(m, CLASSES):
                inside = part[i * TILE : (i + 1) * TILE, (n - m) * TILE : (n - m + 1) * TILE]
                tile = acc[m + i, n] - inside
                acc[m + i, n] = tile
                if n > m + 1:
                    acc[n, m + i] = tile.T
    perm = []
    for k in range(CLASSES):
        place = jnp.int32(0)
        for j in range(1, CLASSES):
            fits = (segments[0, j] & 7) == k
            place = jnp.where(fits, jnp.int32(j), place)
        perm.append(place)
    down = lax.broadcasted_iota(jnp.int32, (TILE, TILE), 0)
    across = lax.broadcasted_iota(jnp.int32, (TILE, TILE), 1)
    copies = []
    for k in range(CLASSES):
        above = down < width[0] - perm[k] * TILE
        for m in range(CLASSES):
            inside = above & (across < width[0] - perm[m] * TILE)
            tile = jnp.where(inside, acc[perm[k], perm[m]], 0.0)
            tiles[k, m % 4, m // 4] = tile
            if k == m:
                diag[k : k + 1, :] = jnp.sum(
                    jnp.where(down == across, tile, 0.0), axis=0, keepdims=True
                )
        copy = pltpu.make_async_copy(tiles.at[k], out.at[k], t_sem.at[k])
        copy.start()
        copies.append(copy)
    for step in range(1, RING):
        pass_on(step).wait()
    for copy in copies:
        copy.wait()


def make_block(coupling, modes, flexibility, width, segments):
    count = modes.shape[1]
    dma = pltpu.SemaphoreType.DMA
    scalars = pl.BlockSpec(memory_space=pltpu.SMEM)
    far, vectors = pl.BlockSpec(memory_space=pltpu.HBM), pl.BlockSpec(memory_space=pltpu.VMEM)
    return pl.pallas_call(
        block_kernel,
        in_specs=[scalars, scalars, far, far, vectors],
        out_specs=[pl.BlockSpec(memory_space=pl.ANY), vectors, vectors],
        out_shape=[
            jax.ShapeDtypeStruct((8, 4, 2, TILE, TILE), F32),
            jax.ShapeDtypeStruct((CLASSES, TILE), F32),
            jax.ShapeDtypeStruct((RING, PLANE, 1, TILE), F32),
        ],
        scratch_shapes=[
            pltpu.VMEM((1, TILE), F32),
            pltpu.VMEM((STEPS, DEPTH, 1024), BF16),
            pltpu.VMEM((count, 4096), BF16),
            pltpu.VMEM((8, 4, 2, TILE, TILE), F32),
            pltpu.VMEM((CLASSES, CLASSES, TILE, TILE), F32),
            pltpu.VMEM((count, 1024), F32),
            dma((STEPS,)),
            dma,
            dma((3,)),
            dma((2, RING - 1)),
            dma((CLASSES,)),
        ],
        compiler_params=pltpu.CompilerParams(
            collective_id=1, has_side_effects=True, vmem_limit_bytes=60 << 20
        ),
        name="block",
    )(segments, width, coupling, modes, flexibility)


def exchange_kernel(cap, table, tiles, diag, ring_out, own_out, diag_out, *scratch):
    chunks = len(PARTS)
    held, send, scratch = scratch[:chunks], scratch[chunks : 2 * chunks], scratch[2 * chunks :]
    spans = [pl.ds(sum(PARTS[:q]), PARTS[q]) for q in range(chunks)]
    diag_held, diag_send, a_send, a_recv, b_send, b_recv, o_sem, d_sem = scratch
    row, col = lax.axis_index("row"), lax.axis_index("col")
    y, z = col // 4, col % 4
    mine = row * 4 + z

    def plane_peer(step):
        there = lax.rem(mine + step, PLANE)
        return there, (there // 4, y * 4 + lax.rem(there, 4))

    def ring_peer(step):
        return (row, lax.rem(y + step, RING) * 4 + z)

    barrier = pltpu.get_barrier_semaphore()

    def greet(step, carry):
        pl.semaphore_signal(barrier, inc=1, device_id=plane_peer(step)[1], device_id_type=MESH)
        return carry

    lax.fori_loop(1, PLANE, greet, 0)
    for step in range(1, RING):
        pl.semaphore_signal(barrier, inc=1, device_id=ring_peer(step), device_id_type=MESH)
    pl.semaphore_wait(barrier, PLANE - 1 + RING - 1)

    own_copies, kept = [None] * chunks, []

    def local(src, dst, sem):
        copy = pltpu.make_async_copy(src, dst, sem)
        copy.start()
        return copy

    def send_diag(step, carry):
        pltpu.make_async_remote_copy(
            src_ref=diag,
            dst_ref=diag_held.at[mine],
            send_sem=d_sem.at[0],
            recv_sem=d_sem.at[1],
            device_id=plane_peer(step)[1],
            device_id_type=MESH,
        ).start()
        return carry

    def start_plane(q):
        def send_tiles(step, carry):
            there, peer = plane_peer(step)
            pltpu.make_async_remote_copy(
                src_ref=tiles.at[there // 4, lax.rem(there, 4), :, spans[q]],
                dst_ref=held[q].at[mine],
                send_sem=a_send.at[q],
                recv_sem=a_recv.at[q],
                device_id=peer,
                device_id_type=MESH,
            ).start()
            return carry

        lax.fori_loop(1, PLANE, send_tiles, 0)
        own_copies[q] = local(tiles.at[row, z, :, spans[q]], held[q].at[mine], o_sem.at[0, q])

    def whole(ref, sem):
        part = ref.at[pl.ds(0, PLANE - 1)]
        pltpu.make_async_copy(part, part, sem).wait()

    pending = []
    for q in range(AHEAD):
        start_plane(q)
    for q in range(chunks):
        whole(held[q], a_recv.at[q])
        own_copies[q].wait()
        for step in range(1, RING):
            parity = lax.rem(y + step, 2)

            def arrange(j, carry, q=q, step=step, parity=parity):
                send[q][step - 1, j] = held[q][table[3 + step, j], parity]
                return carry

            lax.fori_loop(0, cap, arrange, 0)
            copy = pltpu.make_async_remote_copy(
                src_ref=send[q].at[step - 1],
                dst_ref=ring_out.at[step - 1, pl.ds(0, cap), spans[q]],
                send_sem=b_send.at[q, step - 1],
                recv_sem=b_recv.at[q, step - 1],
                device_id=ring_peer(step),
                device_id_type=MESH,
            )
            copy.start()
            pending.append(copy)
        kept.append(local(held[q].at[:, lax.rem(y, 2)], own_out.at[:, spans[q]], o_sem.at[1, q]))
        if q + AHEAD < chunks:
            start_plane(q + AHEAD)
        if q == 1:
            own_diag = local(diag, diag_held.at[mine], d_sem.at[2])
            lax.fori_loop(1, PLANE, send_diag, 0)
        if q == 4:
            whole(diag_held, d_sem.at[1])
            own_diag.wait()

            def pick(i, carry):
                for parity in range(2):
                    diag_send[parity, 0, pl.ds(i, 1), :] = diag_held[i, pl.ds(row, 1), :]
                    diag_send[parity, 1, pl.ds(i, 1), :] = diag_held[i, pl.ds(4 * parity + z, 1), :]
                return carry

            lax.fori_loop(0, PLANE, pick, 0)
            here = local(diag_send.at[lax.rem(y, 2)], diag_out.at[0], d_sem.at[3])
            for step in range(1, RING):
                copy = pltpu.make_async_remote_copy(
                    src_ref=diag_send.at[lax.rem(y + step, 2)],
                    dst_ref=diag_out.at[step],
                    send_sem=b_send.at[chunks, step - 1],
                    recv_sem=b_recv.at[chunks, step - 1],
                    device_id=ring_peer(step),
                    device_id_type=MESH,
                )
                copy.start()
                pending.append(copy)
    for copy in pending:
        copy.wait()
    for copy in kept:
        copy.wait()
    here.wait()
    whole(diag_held, d_sem.at[0])
    for q in range(chunks):
        whole(held[q], a_send.at[q])


def exchange(cap, table, tiles, diag):
    dma = pltpu.SemaphoreType.DMA
    anywhere = pl.BlockSpec(memory_space=pl.ANY)
    return pl.pallas_call(
        functools.partial(exchange_kernel, cap),
        in_specs=[pl.BlockSpec(memory_space=pltpu.SMEM), anywhere, anywhere],
        out_specs=[anywhere] * 3,
        out_shape=[
            jax.ShapeDtypeStruct((RING - 1, PLANE, TILE, TILE), F32),
            jax.ShapeDtypeStruct((PLANE, TILE, TILE), F32),
            jax.ShapeDtypeStruct((RING, 2, PLANE, TILE), F32),
        ],
        scratch_shapes=[pltpu.VMEM((PLANE, 2, part, TILE), F32) for part in PARTS]
        + [pltpu.VMEM((RING - 1, cap, part, TILE), F32) for part in PARTS]
        + [
            pltpu.VMEM((PLANE, CLASSES, TILE), F32),
            pltpu.VMEM((2, 2, PLANE, TILE), F32),
            dma((len(PARTS),)),
            dma((len(PARTS),)),
            dma((len(PARTS) + 1, RING - 1)),
            dma((len(PARTS) + 1, RING - 1)),
            dma((2, len(PARTS))),
            dma((4,)),
        ],
        compiler_params=pltpu.CompilerParams(
            collective_id=cap + 1, has_side_effects=True, vmem_limit_bytes=40 << 20
        ),
        name="exchange",
    )(table, tiles, diag)


def exactly(left, right):
    return lax.dot_general(
        left, right, (((0,), (0,)), ((), ())), precision=HIGH, preferred_element_type=F32
    )


def assemble_kernel(table, ring, own, diag, row_hot, col_hot, out, row_scale, col_scale, acc, sem):
    rows = exactly(diag[:, 0].reshape(RING * PLANE, TILE), row_hot[...])
    cols = exactly(col_hot[...], diag[:, 1].reshape(RING * PLANE, TILE))[:8]
    row_scale[...] = 1.0 / jnp.sqrt(1.0 + jnp.abs(rows))
    col_scale[...] = 1.0 / jnp.sqrt(1.0 + jnp.abs(cols))
    copies = []
    for first in range(0, TILE, SPAN):
        span = slice(first, first + SPAN)
        acc[:, span] = jnp.zeros((ROW_TILES, SPAN, COL_TILES * TILE), F32)
        for d in range(RING):

            def add(j, carry, d=d, span=span):
                code = table[d, j]
                tile = own[code & 31, span] if d == 0 else ring[d - 1, j, span]
                across = pl.ds(pl.multiple_of((code >> 9) * TILE, TILE), TILE)
                acc[(code >> 5) & 15, span, across] += tile
                return carry

            lax.fori_loop(0, table[8 + d, 0], add, 0)
        for g in range(ROW_TILES):
            down = jnp.broadcast_to(row_scale[span, g : g + 1], (SPAN, TILE))
            for h in range(COL_TILES):
                acc[g, span, h * TILE : (h + 1) * TILE] *= down * col_scale[h : h + 1, :]
        copy = pltpu.make_async_copy(acc.at[:, span], out.at[:, span], sem.at[first // SPAN])
        copy.start()
        copies.append(copy)
    for copy in copies:
        copy.wait()


def assemble(table, ring, own, diag, row_hot, col_hot):
    scalars, vectors = pl.BlockSpec(memory_space=pltpu.SMEM), pl.BlockSpec(memory_space=pltpu.VMEM)
    shape = (ROW_TILES, TILE, COL_TILES * TILE)
    return pl.pallas_call(
        assemble_kernel,
        in_specs=[scalars] + [vectors] * 5,
        out_specs=pl.BlockSpec(memory_space=pl.ANY),
        out_shape=jax.ShapeDtypeStruct(shape, F32),
        scratch_shapes=[
            pltpu.VMEM((TILE, TILE), F32),
            pltpu.VMEM((8, TILE), F32),
            pltpu.VMEM(shape, F32),
            pltpu.SemaphoreType.DMA((TILE // SPAN,)),
        ],
        compiler_params=pltpu.CompilerParams(vmem_limit_bytes=24 << 20),
        name="assemble",
    )(table, ring, own, diag, row_hot, col_hot)


def places_kernel(segments, all_wide, table, row_hot, col_hot, choice, plane, tags):
    row, col = lax.axis_index("row"), lax.axis_index("col")
    y, z = col // 4, col % 4
    lane = lax.broadcasted_iota(jnp.int32, (PLANE, TILE), 1)
    slot = lax.broadcasted_iota(jnp.int32, (PLANE, TILE), 0)
    lane8 = lax.broadcasted_iota(jnp.int32, (PLANE, CLASSES), 1)
    need = jnp.zeros((CLASSES, TILE), F32)
    half = lax.broadcasted_iota(jnp.int32, (CLASSES, TILE), 0) >> 2
    for p in range(RING):
        for k in range(CLASSES):
            first = 16 * k + 4 * p
            plane[p, 4 * k : 4 * k + 4, :] = segments[first : first + 4, :]
        numbers = plane[p]
        width = all_wide[p, :, 0, :].astype(jnp.int32)
        tag = jnp.zeros((PLANE, TILE), jnp.int32)
        for k in range(CLASSES):
            found = jnp.where((numbers & 7) == k, numbers + 128 * lane8, 0)
            found = jnp.broadcast_to(jnp.sum(found, axis=1, keepdims=True), (PLANE, TILE))
            used = jnp.where((found >> 7) * TILE < width, 128, 0)
            tag = jnp.where(lane == k, (found & 127) + used, tag)
        tags[p] = tag
        filled = (tag >> 7).astype(F32)
        high = ((tag >> 3) & 1).astype(F32)
        for h, part in ((0, filled * (1.0 - high)), (1, filled * high)):
            held = over_rows(part, filled)[:CLASSES]
            need = jnp.maximum(need, jnp.where(2 * h + half == p, 0.0, held))

    def column(values, index):
        picked = jnp.sum(jnp.where(lane == index, values, 0), axis=1, keepdims=True)
        return jnp.broadcast_to(picked, (PLANE, TILE))

    earlier = lax.broadcasted_iota(jnp.int32, (PLANE, PLANE), 0) > lax.broadcasted_iota(
        jnp.int32, (PLANE, PLANE), 1
    )
    earlier = jnp.where(earlier, 1.0, 0.0).astype(F32)

    def listed(flag, values):
        rank = jnp.dot(earlier, jnp.where(flag, 1.0, 0.0), preferred_element_type=F32)
        lands = flag & (rank.astype(jnp.int32) == lane)
        return jnp.sum(jnp.where(lands, values, 0), axis=0, keepdims=True)

    table[...] = jnp.zeros((16, TILE), jnp.int32)
    here = tags[y]
    mine = column(here, row)
    for d in range(RING):
        tag = tags[(y - d) & 3]
        down, across = column(tag, row), column(tag, col & 7)
        owned = ((across >> 3) & 1) == (col >> 3)
        arrives = owned & (down > 127) & (across > 127)
        code = slot + 32 * ((down & 127) >> 3) + 512 * ((across & 127) >> 4)
        table[d : d + 1, :] = listed(arrives, code)
        table[8 + d : 9 + d, :] = jnp.sum(jnp.where(arrives, 1, 0), axis=0, keepdims=True)
        rows = slice(d * PLANE, (d + 1) * PLANE)
        row_hot[rows, :] = jnp.where(((down & 127) >> 3) == lane, 1.0, 0.0)
        col_hot[rows, :] = jnp.where(owned & (((across & 127) >> 4) == lane), 1.0, 0.0)
        if d:
            goes = (y + d) & 3
            out = column(here, 4 * (goes & 1) + z)
            leaves = (((out >> 3) & 1) == (goes >> 1)) & (out > 127) & (mine > 127)
            table[3 + d : 4 + d, :] = listed(leaves, slot)
    most = jnp.max(need).astype(jnp.int32)
    level = 0
    for cap in CAPS[:-1]:
        level = level + jnp.where(most > cap, jnp.int32(1), jnp.int32(0))
    choice[0] = level


def places(segments, all_wide):
    vectors = pl.BlockSpec(memory_space=pltpu.VMEM)
    return pl.pallas_call(
        places_kernel,
        in_specs=[vectors] * 2,
        out_specs=[vectors] * 3 + [pl.BlockSpec(memory_space=pltpu.SMEM)],
        out_shape=[
            jax.ShapeDtypeStruct((16, TILE), jnp.int32),
            jax.ShapeDtypeStruct((RING * PLANE, TILE), F32),
            jax.ShapeDtypeStruct((RING * PLANE, TILE), F32),
            jax.ShapeDtypeStruct((1,), jnp.int32),
        ],
        scratch_shapes=[
            pltpu.VMEM((RING, PLANE, CLASSES), jnp.int32),
            pltpu.VMEM((RING, PLANE, TILE), jnp.int32),
        ],
        name="places",
    )(segments, all_wide)


def body(coupling, modes, flexibility, widths, segments):
    device = lax.axis_index("row") * 16 + lax.axis_index("col")
    own_segments = lax.dynamic_slice_in_dim(segments, device, 1, 0)
    tiles, diag, all_wide = make_block(coupling, modes, flexibility, widths, own_segments)
    table, row_hot, col_hot, choice = places(segments, all_wide)
    ring, own, diags = lax.switch(
        choice[0], [functools.partial(exchange, cap) for cap in CAPS], table, tiles, diag
    )
    out = assemble(table, ring, own, diags, row_hot, col_hot)
    return out.reshape(ROW_TILES * TILE, COL_TILES * TILE)


def solution(mesh):
    both = ("row", "col")
    return jax.shard_map(
        body,
        mesh=mesh,
        in_specs=(P(both, None, None), P(both, None, None), P(both, None), P(both), P()),
        out_specs=P("row", "col"),
        check_vma=False,
    )
```

profile of v0, /device:TPU:6, one launch (start us, length us, event | category | flops | bytes accessed | tf_op | source)
XLA Modules:
  0.0 107.6 jit_solution(15539982691428865781)
XLA Ops:
  0.7 0.8 copy.7.segments
  1.4 0.0 copy-start.2
  1.4 0.6 constant_dynamic-slice_fusion.segments
  2.0 19.0 %block.1 = (f32[8,4,2,128,128]{4,3,2,1,0:T(8,128)}, f32[8,128]{1,0:T(8,128)S(1)}, f32[4,32,1,128]{3,2,1,0:T(1,128)}) custom-call(s32[1,8]{1,0:T(1,128)} %constant_dynamic-slice_fusion.segments, s32[1]{0:T(128)S(6)} %copy.29.width, bf16[1,4096,1024]{2,1,0:T(8,128)(2,1)} %coupling.1, bf16[1,200,4096]{2,1,0:T(8,128)(2,1)} %modes.1, f32[1,200]{1,0:T(1,128)} %weights.1), custom_call_target="tpu_custom_call" | custom-call | tf_op jit(solution)/shard_map/block/pallas_call | solution.py:175
  21.0 0.0 copy-done.2
  21.1 2.3 %places.1 = (s32[16,128]{1,0:T(8,128)S(1)}, f32[128,128]{1,0:T(8,128)}, f32[128,128]{1,0:T(8,128)}, s32[1]{0:T(128)}) custom-call(s32[128,8]{1,0:T(8,128)} %copy-done.2, f32[4,32,1,128]{3,2,1,0:T(1,128)} %get-tuple-element.78.all_wide), custom_call_target="tpu_custom_call" | custom-call | tf_op jit(solution)/shard_map/places/pallas_call | solution.py:487
  24.0 0.0 copy-start
  24.0 0.0 copy-start.1
  24.0 77.3 %conditional.1 = ((f32[3,32,128,128]{3,2,1,0:T(8,128)}, f32[32,128,128]{2,1,0:T(8,128)S(1)}, f32[4,2,32,128]{3,2,1,0:T(8,128)S(1)})) conditional(s32[]{:T(128)} %bitcast, (s32[16,128]{1,0:T(8,128)S(1)}, f32[8,4,2,128,128]{4,3,2,1,0:T(8,128)}, f32[8,128]{1,0:T(8,128)S(1)}) %tuple.26, (s32[16,128]{1,0:T(8,128)S(1)}, ...), branch_computations={%region_0.0_spmd, %region_1.0_spmd, %region_2.0_spmd, %region_3.0_... | conditional | bytes 8 | solution.py:510
  24.1 77.3 %exchange.9 = (f32[3,32,128,128]{3,2,1,0:T(8,128)}, f32[32,128,128]{2,1,0:T(8,128)S(1)}, f32[4,2,32,128]{3,2,1,0:T(8,128)S(1)}) custom-call(s32[16,128]{1,0:T(8,128)S(1)} %get-tuple-element.53.table, f32[8,4,2,128,128]{4,3,2,1,0:T(8,128)} %get-tuple-element.54.tiles, f32[8,128]{1,0:T(8,128)S(1)} %get-tuple-element.55.diag), custom_call_target="tpu_custom_call" | custom-call | tf_op jit(solution)/shard_map/cond/branch_2_fun/exchange/pallas_call | solution.py:335
  101.4 0.0 copy-done
  101.4 0.0 copy-done.1
  101.4 6.2 %assemble.1 = f32[12,128,768]{2,1,0:T(8,128)} custom-call(s32[16,128]{1,0:T(8,128)S(1)} %get-tuple-element.79.table, f32[3,32,128,128]{3,2,1,0:T(8,128)} %get-tuple-element.83.ring, f32[32,128,128]{2,1,0:T(8,128)S(1)} %get-tuple-element.84.own, f32[4,2,32,128]{3,2,1,0:T(8,128)S(1)} %get-tuple-element.85.diag, f32[128,128]{1,0:T(8,128)S(1)} %copy-done, ...), custom_call_target="tpu_custom_call" | custom-call | tf_op jit(solution)/shard_map/assemble/pallas_call | solution.py:402
Async XLA Ops:
  1.4 19.6 %copy-start.2 = (s32[128,8]{1,0:T(8,128)}, s32[128,8]{1,0:T(8,128)S(1)}, u32[]{:S(2)}) copy-start(s32[128,8]{1,0:T(8,128)S(1)} %copy.7.segments) | copy-start | bytes 12292
  24.0 77.4 %copy-start = (f32[128,128]{1,0:T(8,128)S(1)}, f32[128,128]{1,0:T(8,128)}, u32[]{:S(2)}) copy-start(f32[128,128]{1,0:T(8,128)} %get-tuple-element.86.row_hot) | copy-start | bytes 196612
  24.0 77.4 %copy-start.1 = (f32[128,128]{1,0:T(8,128)S(1)}, f32[128,128]{1,0:T(8,128)}, u32[]{:S(2)}) copy-start(f32[128,128]{1,0:T(8,128)} %get-tuple-element.87.col_hot) | copy-start | bytes 196612
where the time goes:
time: 108 us
  Pallas kernels  105 us (97%)
  local copies, waits for them, and re-layouts  1.39 us (1%)
  between operations  1.34 us (1%)
    pallas_call x1, Pallas kernels, exchange(): pl.pallas_call(functools.partial(exchange_kernel, cap), in_specs=[pl.Bloc...  77.3 us
    pallas_call x1, Pallas kernels, make_block(): pl.pallas_call(block_kernel, in_specs=[scalars, scalars, far, far, vector...  19 us
    pallas_call x1, Pallas kernels, assemble(): pl.pallas_call(assemble_kernel, in_specs=[scalars] + [vectors] * 5, out_s...  6.19 us
    pallas_call x1, Pallas kernels, places(): pl.pallas_call(places_kernel, in_specs=[vectors] * 2, out_specs=[vectors]...  2.35 us

commit v1 on v0

--- a/solution.py
+++ b/solution.py
@@ -18,7 +18,7 @@
 DEPTH = 1024
 STEPS = 4
 SPAN = 64
-CAPS = (17, 18, 19, 20, 21, 23, PLANE)
+CAPS = (17, 18, 19, 20, 21, 22, 25, PLANE)
 F32 = jnp.float32
 BF16 = jnp.bfloat16
 MESH = pl.DeviceIdType.MESH

time: 108 us -> 107 us (level); the launches traced: 108 us -> 105 us
  Pallas kernels: 105 us -> 102 us
    pallas_call x1, Pallas kernels: 77.3 us -> 74.4 us  [exchange(): pl.pallas_call(functools.partial(exchange_kernel, cap), in_specs=[pl.Bloc...]
where the time goes in v1:
time: 107 us; the launch traced here: 105 us
  Pallas kernels  102 us (95%)
  local copies, waits for them, and re-layouts  1.39 us (1%)
  between operations  1.34 us (1%)
    pallas_call x1, Pallas kernels, exchange(): pl.pallas_call(functools.partial(exchange_kernel, cap), in_specs=[pl.Bloc...  74.4 us
    pallas_call x1, Pallas kernels, make_block(): pl.pallas_call(block_kernel, in_specs=[scalars, scalars, far, far, vector...  19 us
    pallas_call x1, Pallas kernels, assemble(): pl.pallas_call(assemble_kernel, in_specs=[scalars] + [vectors] * 5, out_s...  6.31 us
    pallas_call x1, Pallas kernels, places(): pl.pallas_call(places_kernel, in_specs=[vectors] * 2, out_specs=[vectors]...  2.35 us

profile of v1, /device:TPU:6, one launch (start us, length us, event | category | flops | bytes accessed | tf_op | source)
XLA Modules:
  0.0 104.9 jit_solution(3038244584404510595)
XLA Ops:
  0.7 0.8 copy.7.segments
  1.4 0.0 copy-start.2
  1.4 0.6 constant_dynamic-slice_fusion.segments
  2.0 19.0 %block.1 = (f32[8,4,2,128,128]{4,3,2,1,0:T(8,128)}, f32[8,128]{1,0:T(8,128)S(1)}, f32[4,32,1,128]{3,2,1,0:T(1,128)}) custom-call(s32[1,8]{1,0:T(1,128)} %constant_dynamic-slice_fusion.segments, s32[1]{0:T(128)S(6)} %copy.32.width, bf16[1,4096,1024]{2,1,0:T(8,128)(2,1)} %coupling.1, bf16[1,200,4096]{2,1,0:T(8,128)(2,1)} %modes.1, f32[1,200]{1,0:T(1,128)} %weights.1), custom_call_target="tpu_custom_call" | custom-call | tf_op jit(solution)/shard_map/block/pallas_call | solution.py:175
  21.0 0.0 copy-done.2
  21.1 2.3 %places.1 = (s32[16,128]{1,0:T(8,128)S(1)}, f32[128,128]{1,0:T(8,128)}, f32[128,128]{1,0:T(8,128)}, s32[1]{0:T(128)}) custom-call(s32[128,8]{1,0:T(8,128)} %copy-done.2, f32[4,32,1,128]{3,2,1,0:T(1,128)} %get-tuple-element.87.all_wide), custom_call_target="tpu_custom_call" | custom-call | tf_op jit(solution)/shard_map/places/pallas_call | solution.py:487
  24.0 0.0 copy-start
  24.0 0.0 copy-start.1
  24.0 74.5 %conditional.1 = ((f32[3,32,128,128]{3,2,1,0:T(8,128)}, f32[32,128,128]{2,1,0:T(8,128)S(1)}, f32[4,2,32,128]{3,2,1,0:T(8,128)S(1)})) conditional(s32[]{:T(128)} %bitcast, (s32[16,128]{1,0:T(8,128)S(1)}, f32[8,4,2,128,128]{4,3,2,1,0:T(8,128)}, f32[8,128]{1,0:T(8,128)S(1)}) %tuple.29, (s32[16,128]{1,0:T(8,128)S(1)}, ...), branch_computations={%region_0.0_spmd, %region_1.0_spmd, %region_2.0_spmd, %region_3.0_... | conditional | bytes 8 | solution.py:510
  24.1 74.4 %exchange.9 = (f32[3,32,128,128]{3,2,1,0:T(8,128)}, f32[32,128,128]{2,1,0:T(8,128)S(1)}, f32[4,2,32,128]{3,2,1,0:T(8,128)S(1)}) custom-call(s32[16,128]{1,0:T(8,128)S(1)} %get-tuple-element.56.table, f32[8,4,2,128,128]{4,3,2,1,0:T(8,128)} %get-tuple-element.57.tiles, f32[8,128]{1,0:T(8,128)S(1)} %get-tuple-element.58.diag), custom_call_target="tpu_custom_call" | custom-call | tf_op jit(solution)/shard_map/cond/branch_1_fun/exchange/pallas_call | solution.py:335
  98.5 0.0 copy-done
  98.5 0.0 copy-done.1
  98.5 6.3 %assemble.1 = f32[12,128,768]{2,1,0:T(8,128)} custom-call(s32[16,128]{1,0:T(8,128)S(1)} %get-tuple-element.88.table, f32[3,32,128,128]{3,2,1,0:T(8,128)} %get-tuple-element.92.ring, f32[32,128,128]{2,1,0:T(8,128)S(1)} %get-tuple-element.93.own, f32[4,2,32,128]{3,2,1,0:T(8,128)S(1)} %get-tuple-element.94.diag, f32[128,128]{1,0:T(8,128)S(1)} %copy-done, ...), custom_call_target="tpu_custom_call" | custom-call | tf_op jit(solution)/shard_map/assemble/pallas_call | solution.py:402
Async XLA Ops:
  1.4 19.6 %copy-start.2 = (s32[128,8]{1,0:T(8,128)}, s32[128,8]{1,0:T(8,128)S(1)}, u32[]{:S(2)}) copy-start(s32[128,8]{1,0:T(8,128)S(1)} %copy.7.segments) | copy-start | bytes 12292
  24.0 74.5 %copy-start = (f32[128,128]{1,0:T(8,128)S(1)}, f32[128,128]{1,0:T(8,128)}, u32[]{:S(2)}) copy-start(f32[128,128]{1,0:T(8,128)} %get-tuple-element.95.row_hot) | copy-start | bytes 196612
  24.0 74.5 %copy-start.1 = (f32[128,128]{1,0:T(8,128)S(1)}, f32[128,128]{1,0:T(8,128)}, u32[]{:S(2)}) copy-start(f32[128,128]{1,0:T(8,128)} %get-tuple-element.96.col_hot) | copy-start | bytes 196612
